TPU v7x, 256 devices: a whole 4x4x8 slice. The times are simulated.
256 devices in a mesh: row: 8 (over y, core), col: 16 (over z_hi, x), layer: 2 (over z_lo).
Axes of the slice: x: 4, y: 4, z: 8 (z_hi: 4, z_lo: 2; z = z_hi * 2 + z_lo), core: 2. Of those that a mesh axis runs over, the one named last changes fastest.
Arguments:
- tile_values: float32 [8, 32, 2, 6, 128, 128], P('row', ('col', 'layer')), may hold values from -1.8 to 1.8
- tile_rows: int32 [8, 32, 2, 6], P('row', ('col', 'layer')), may hold values from 0 to 255, as said below
- tile_cols: int32 [8, 32, 2, 6], P('row', ('col', 'layer')), may hold values from 0 to 255, as said below
- tile_counts: int32 [8, 32, 2], P('row', ('col', 'layer')), may hold values from 1 to 6, as said below
- out_rows: int32 [8, 16, 2, 12], P('row', 'col'), may hold values from 0 to 255, as said below
- out_cols: int32 [8, 16, 2, 12], P('row', 'col'), may hold values from 0 to 255, as said below
Outputs:
- squared: float32 [8, 32, 12, 128, 128], P('row', ('col', 'layer'))
Inputs may be any that keep to these rules, and one draw needn't show every extreme that they name: `tile_rows`: entry [r, s, h, q] lies in row band r (the 32 block rows from r * 32), in a run of 8 block rows whose index is congruent to h modulo 2; within one list [r, s, h] the 6 slots have distinct rows. `tile_cols`: entry [r, s, h, q] lies in sub-band s: block columns s * 8 to s * 8 + 7. Slots q < tile_counts[r, s, h] of list [r, s, h] hold tiles; values and coordinates in later slots mean nothing. Some list holds 6 tiles in every draw. out_rows[r, c, l, o] and out_cols[r, c, l, o] place the o-th kept tile of row band r and sub-band c * 2 + l; the row lies in row band r, the column in that sub-band, and the 12 positions of one [r, c, l] are distinct. `out_cols`: see out_rows.
All inputs are finite; a program needn't handle non-finite values.
Results may differ from a plain program's by a relative error of at most 0.0003.
Values sent between devices are 32-bit elements; how exact they have to be, the bound alone decides.
No kernel may reach another device: no remote copies, remote signals or barrier semaphores. Data moves between devices by JAX's collectives and lax.ppermute only.
A program may use at most 128 MiB of HBM per device.

v0:
```python
import jax
import jax.numpy as jnp
from jax import lax
from jax.sharding import PartitionSpec as P


def live_slots(counts, capacity):
    slot_ids = jnp.arange(capacity, dtype=jnp.int32)
    return slot_ids < counts[..., None]


def flatten_list(listed):
    values, list_rows, list_cols, counts = listed
    tile_order = values.shape[-1]
    capacity = values.shape[-3]
    live_mask = live_slots(counts, capacity)
    return (
        values.reshape(-1, tile_order, tile_order),
        list_rows.reshape(-1),
        list_cols.reshape(-1),
        live_mask.reshape(-1),
    )


def tile_products(running, one_shard, column_panel, target_rows, target_cols):
    left_values, left_rows, left_cols, left_live = one_shard
    right_values, right_rows, right_cols, right_live = column_panel
    left_hits = (left_live[None, :] & (left_rows[None, :] == target_rows[:, None])).astype(
        jnp.int32
    )
    left_pick = jnp.argmax(left_hits, axis=1)
    inner_index = jnp.take(left_cols, left_pick)
    right_hits = (
        right_live[None, :]
        & (right_rows[None, :] == inner_index[:, None])
        & (right_cols[None, :] == target_cols[:, None])
    ).astype(jnp.int32)
    right_pick = jnp.argmax(right_hits, axis=1)
    weight = (jnp.max(left_hits, axis=1) * jnp.max(right_hits, axis=1)).astype(jnp.float32)
    left_tiles = jnp.take(left_values, left_pick, axis=0)
    right_tiles = jnp.take(right_values, right_pick, axis=0)
    products = jnp.einsum(
        "opq,oqr->opr",
        left_tiles,
        right_tiles,
        precision=lax.Precision.HIGHEST,
        preferred_element_type=jnp.float32,
    )
    return running + products * weight[:, None, None]


def column_panel_of(listed):
    return flatten_list(lax.all_gather(listed, "row", axis=0, tiled=True))


def fold_over(column_panel, target_rows, target_cols, running, arrived):
    values, piece_rows, piece_cols, counts = arrived
    pieces_count = values.shape[1]
    tile_order = values.shape[-1]
    capacity = values.shape[-3]
    live_mask = live_slots(counts, capacity)
    shards = (
        values.reshape(pieces_count, -1, tile_order, tile_order),
        piece_rows.reshape(pieces_count, -1),
        piece_cols.reshape(pieces_count, -1),
        live_mask.reshape(pieces_count, -1),
    )

    def advance(carried, one_shard):
        return (tile_products(carried, one_shard, column_panel, target_rows, target_cols), None)

    running, unused = lax.scan(advance, running, shards)
    return running


def local(tile_values, tile_rows, tile_cols, tile_counts, out_rows, out_cols):
    tile_order = tile_values.shape[-1]
    own_list = (tile_values, tile_rows, tile_cols, tile_counts)
    column_panel = column_panel_of(own_list)
    layer_index = lax.axis_index("layer")
    target_rows = lax.dynamic_index_in_dim(out_rows[0, 0], layer_index, 0, keepdims=False)
    target_cols = lax.dynamic_index_in_dim(out_cols[0, 0], layer_index, 0, keepdims=False)
    empty_sums = jnp.zeros((target_rows.shape[0], tile_order, tile_order), jnp.float32)
    summed = fold_over(
        column_panel,
        target_rows,
        target_cols,
        empty_sums,
        (
            lax.all_gather(own_list[0], ("col", "layer"), axis=1, tiled=True),
            lax.all_gather(own_list[1], ("col", "layer"), axis=1, tiled=True),
            lax.all_gather(own_list[2], ("col", "layer"), axis=1, tiled=True),
            lax.all_gather(own_list[3], ("col", "layer"), axis=1, tiled=True),
        ),
    )
    result = summed.reshape(1, 1, -1, tile_order, tile_order)
    return result


def solution(mesh):
    in_specs = (
        P("row", ("col", "layer"), None, None, None, None),
        P("row", ("col", "layer"), None, None),
        P("row", ("col", "layer"), None, None),
        P("row", ("col", "layer"), None),
        P("row", "col", None, None),
        P("row", "col", None, None),
    )
    out_specs = P("row", ("col", "layer"), None, None, None)
    return jax.shard_map(local, mesh=mesh, in_specs=in_specs, out_specs=out_specs, check_vma=False)
```

profile of v0, /device:TPU:1, one launch (start us, length us, event | category | flops | bytes accessed | tf_op | source)
XLA Modules:
  0.0 899.1 jit_solution(16524936345030754830)
XLA Ops:
  8.0 12.2 %all_gather.27 = s32[8,1,2]{2,1,0:T(1,128)S(1)} all-gather(s32[1,1,2]{2,1,0:T(1,128)} %param.11), channel_id=1, replica_groups=mesh['row'=8,'col'=16,'layer'=2] {'row'}, dimensions={0}, use_global_device_ids=true | all-gather | bytes 72 | tf_op jit(solution)/shard_map/all_gather | solution.py:53
  20.2 8.8 all_gather.30
  29.1 9.3 %all_gather.28 = s32[8,1,2,6]{3,2,1,0:T(2,128)S(1)} all-gather(s32[1,1,2,6]{3,2,1,0:T(2,128)} %param.9), channel_id=1, replica_groups=mesh['row'=8,'col'=16,'layer'=2] {'row'}, dimensions={0}, use_global_device_ids=true | all-gather | bytes 432 | tf_op jit(solution)/shard_map/all_gather | solution.py:53
  38.5 64.3 %all_gather.25 = s32[1,32,2,6]{3,2,0,1:T(2,128)S(1)} all-gather(s32[1,1,2,6]{3,2,0,1:T(2,128)} %bitcast.52), channel_id=1, replica_groups=mesh['row'=8,'col'=16,'layer'=2] {'col','layer'}, dimensions={1}, use_global_device_ids=true | all-gather | bytes 1584 | tf_op jit(solution)/shard_map/all_gather | solution.py:91
  103.0 58.1 %all_gather.29 = s32[1,32,2,6]{3,2,0,1:T(2,128)S(1)} all-gather(s32[1,1,2,6]{3,2,0,1:T(2,128)} %bitcast.53), channel_id=1, replica_groups=mesh['row'=8,'col'=16,'layer'=2] {'col','layer'}, dimensions={1}, use_global_device_ids=true | all-gather | bytes 1584 | tf_op jit(solution)/shard_map/all_gather | solution.py:92
  161.2 57.5 %all_gather.24 = s32[1,32,2]{2,0,1:T(1,128)S(1)} all-gather(s32[1,1,2]{2,0,1:T(1,128)} %bitcast.55), channel_id=1, replica_groups=mesh['row'=8,'col'=16,'layer'=2] {'col','layer'}, dimensions={1}, use_global_device_ids=true | all-gather | bytes 264 | tf_op jit(solution)/shard_map/all_gather | solution.py:93
  219.7 377.2 %all-gather.3.cloned.1.call-done = f32[1,32,2,6,128,128]{5,4,3,2,0,1:T(8,128)} async-done(((f32[1,1,2,6,128,128]{5,4,3,2,0,1:T(8,128)}), f32[1,32,2,6,128,128]{5,4,3,2,0,1:T(8,128)}) %all-gather.3.cloned.1.call-update) | async-done | bytes 25165840 | tf_op jit(solution)/shard_map/all_gather | solution.py:90
  596.9 294.5 %while.12 = (s32[]{:T(128)}, f32[12,128,128]{2,1,0:T(8,128)S(1)}, pred[32,12]{1,0:T(8,128)(4,1)S(1)}, s32[32,12]{1,0:T(8,128)S(1)}, s32[12]{0:T(128)S(1)}, /*ind...) while((s32[]{:T(128)}, f32[12,128,128]{2,1,0:T(8,128)S(1)}, ...), condition=%wide.wide.region_5.6_spmd.clone, body=%wide.wide.region_0.5_spmd.clone.sunk | while | flops 302997888 | bytes 7876635 | solution.py:72
  599.3 3.4 gather_fusion.1
  608.5 3.4 gather_fusion.1
  617.8 3.4 gather_fusion.1
  627.0 3.4 gather_fusion.1
  636.2 3.4 gather_fusion.1
  645.4 3.4 gather_fusion.1
  654.6 3.4 gather_fusion.1
  663.8 3.4 gather_fusion.1
  673.0 3.4 gather_fusion.1
  682.2 3.4 gather_fusion.1
  691.4 3.4 gather_fusion.1
  700.6 3.4 gather_fusion.1
  709.8 3.4 gather_fusion.1
  719.0 3.4 gather_fusion.1
  728.2 3.4 gather_fusion.1
  737.4 3.4 gather_fusion.1
  746.6 3.4 gather_fusion.1
  755.8 3.4 gather_fusion.1
  765.0 3.4 gather_fusion.1
  774.2 3.4 gather_fusion.1
  783.4 3.4 gather_fusion.1
  792.6 3.4 gather_fusion.1
  801.8 3.4 gather_fusion.1
  884.7 3.4 gather_fusion.1
  (640 shorter events, 214.6 us)
Async XLA Ops:
  6.5 213.2 %all-gather.5.cloned.1.call-start = ((), (), s32[]{:S(2)}) async-start(), calls=%async_computation.1 | async-start | bytes 7077888 | tf_op jit(solution)/shard_map/all_gather | solution.py:53
  7.3 589.6 %all-gather.3.cloned.1.call-start = ((), (), s32[]{:S(2)}) async-start(), calls=%async_computation | async-start | bytes 25952256 | tf_op jit(solution)/shard_map/all_gather | solution.py:90
  29.0 567.9 %copy-start.1 = (s32[8,1,2,6]{3,2,1,0:T(2,128)}, s32[8,1,2,6]{3,2,1,0:T(2,128)S(1)}, u32[]{:S(2)}) copy-start(s32[8,1,2,6]{3,2,1,0:T(2,128)S(1)} %all_gather.30) | copy-start | bytes 1156
  38.4 558.5 %copy-start.2 = (s32[8,1,2,6]{3,2,1,0:T(2,128)}, s32[8,1,2,6]{3,2,1,0:T(2,128)S(1)}, u32[]{:S(2)}) copy-start(s32[8,1,2,6]{3,2,1,0:T(2,128)S(1)} %all_gather.28) | copy-start | bytes 1156
  891.4 0.9 copy-start
Sparse Core Ops, SparseCore 0:
  9.2 47.7 all-gather.4
  58.8 538.0 all-gather.2
where the time goes:
time: 902 us; the launch traced here: 899 us
  waiting for transfers between devices  379 us (42%)
  blocking collectives  210 us (23%)
  local copies, waits for them, and re-layouts  193 us (21%)
  other arithmetic  65.1 us (7%)
  matrix products  36.4 us (4%)
  between operations  13.4 us (1%)
    all_gather x1, waiting for transfers between devices, local(): lax.all_gather(own_list[0], ('col', 'layer'), axis=1, tiled=True)  377 us
    gather x32, local copies, waits for them, and re-layouts, tile_products(): right_tiles = jnp.take(right_values, right_pick, axis=0)  108 us
    all_gather x1, blocking collectives, local(): lax.all_gather(own_list[1], ('col', 'layer'), axis=1, tiled=True)  64.3 us
    all_gather x1, blocking collectives, local(): lax.all_gather(own_list[2], ('col', 'layer'), axis=1, tiled=True)  58.1 us
    all_gather x1, blocking collectives, local(): lax.all_gather(own_list[3], ('col', 'layer'), axis=1, tiled=True)  57.5 us
    squeeze x32, local copies, waits for them, and re-layouts, fold_over(): running, unused = lax.scan(advance, running, shards)  38.1 us
    dot_general x32, matrix products, tile_products(): jnp.einsum('opq,oqr->opr', left_tiles, right_tiles, precision=lax.Precisi...  36.4 us
    all_gather x3, blocking collectives, column_panel_of(): return flatten_list(lax.all_gather(listed, 'row', axis=0, tiled=True))  30.3 us
  transfers between devices with their start and end apart: 2, of which 1 were waited for; matrix products, arithmetic and copies ran while one was open for 0% of the time, Pallas kernels for 0%

commit v1 on v0

--- a/solution.py
+++ b/solution.py
@@ -89,7 +89,15 @@
         (
             lax.all_gather(own_list[0], ("col", "layer"), axis=1, tiled=True),
             lax.all_gather(own_list[1], ("col", "layer"), axis=1, tiled=True),
-            lax.all_gather(own_list[2], ("col", "layer"), axis=1, tiled=True),
+            jnp.concatenate(
+                lax.all_to_all(
+                    jnp.stack([own_list[2]] * lax.axis_size(("col", "layer"))),
+                    ("col", "layer"),
+                    0,
+                    0,
+                ),
+                axis=1,
+            ),
             lax.all_gather(own_list[3], ("col", "layer"), axis=1, tiled=True),
         ),
     )

time: 902 us -> 897 us (level)
  blocking collectives: 210 us -> 161 us
  waiting for transfers between devices: 379 us -> 414 us
  starting transfers between devices: 0.04 us -> 11.9 us
    all_gather x1 -> x0, blocking collectives: 58.1 us -> none  [local(): lax.all_gather(own_list[2], ('col', 'layer'), axis=1, tiled=True)]
    all_gather x1, waiting for transfers between devices: 377 us -> 413 us  [local(): lax.all_gather(own_list[0], ('col', 'layer'), axis=1, tiled=True)]
    all_gather x3, blocking collectives: 30.3 us -> 43.4 us  [column_panel_of(): return flatten_list(lax.all_gather(listed, 'row', axis=0, tiled=True))]
    all_to_all x0 -> x1, starting transfers between devices: none -> 11.9 us  [local(): lax.all_to_all(jnp.stack([own_list[2]] * lax.axis_size(('col', 'layer')))...]
  transfers between devices with their start and end apart: 2 -> 3, of which waited for: 1 -> 1; matrix products, arithmetic and copies ran while one was open for 0% -> 0% of each run, Pallas kernels for 0% -> 0%
where the time goes in v1:
time: 897 us; the launch traced here: 894 us
  waiting for transfers between devices  414 us (46%)
  local copies, waits for them, and re-layouts  194 us (22%)
  blocking collectives  161 us (18%)
  other arithmetic  60.9 us (7%)
  matrix products  36.4 us (4%)
  between operations  13.4 us (1%)
  starting transfers between devices  11.9 us (1%)
    all_gather x1, waiting for transfers between devices, local(): lax.all_gather(own_list[0], ('col', 'layer'), axis=1, tiled=True)  413 us
    gather x32, local copies, waits for them, and re-layouts, tile_products(): right_tiles = jnp.take(right_values, right_pick, axis=0)  108 us
    all_gather x1, blocking collectives, local(): lax.all_gather(own_list[3], ('col', 'layer'), axis=1, tiled=True)  59.4 us
    all_gather x1, blocking collectives, local(): lax.all_gather(own_list[1], ('col', 'layer'), axis=1, tiled=True)  58.2 us
    all_gather x3, blocking collectives, column_panel_of(): return flatten_list(lax.all_gather(listed, 'row', axis=0, tiled=True))  43.4 us
    squeeze x32, local copies, waits for them, and re-layouts, fold_over(): running, unused = lax.scan(advance, running, shards)  38.1 us
    dot_general x32, matrix products, tile_products(): jnp.einsum('opq,oqr->opr', left_tiles, right_tiles, precision=lax.Precisi...  36.4 us
    another operation x32, other arithmetic, tile_products(): right_pick = jnp.argmax(right_hits, axis=1)  22.5 us
  transfers between devices with their start and end apart: 3, of which 1 were waited for; matrix products, arithmetic and copies ran while one was open for 0% of the time, Pallas kernels for 0%

profile of v1, /device:TPU:1, one launch (start us, length us, event | category | flops | bytes accessed | tf_op | source)
XLA Modules:
  0.0 894.3 jit_solution(4937947733133689669)
XLA Ops:
  9.3 11.9 %all-to-all-start = ((s32[32,1,1,2,6]{4,3,2,1,0:T(2,128)}), s32[32,1,1,2,6]{4,3,2,1,0:T(2,128)S(1)}, u32[]{:S(2)}, u32[]{:S(2)}) async-start(s32[32,1,1,2,6]{4,3,2,1,0:T(2,128)} %stack.2), calls=%async_computation | async-start | bytes 65536 | tf_op jit(solution)/shard_map/all_to_all | solution.py:93
  21.2 59.4 %all_gather.21 = s32[1,32,2]{2,0,1:T(1,128)S(1)} all-gather(s32[1,1,2]{2,0,1:T(1,128)} %bitcast.53), channel_id=1, replica_groups=mesh['row'=8,'col'=16,'layer'=2] {'col','layer'}, dimensions={1}, use_global_device_ids=true | all-gather | bytes 264 | tf_op jit(solution)/shard_map/all_gather | solution.py:101
  81.5 25.3 %all_gather.24 = s32[8,1,2]{2,1,0:T(1,128)S(1)} all-gather(s32[1,1,2]{2,1,0:T(1,128)} %param.11), channel_id=1, replica_groups=mesh['row'=8,'col'=16,'layer'=2] {'row'}, dimensions={0}, use_global_device_ids=true | all-gather | bytes 72 | tf_op jit(solution)/shard_map/all_gather | solution.py:53
  106.8 8.4 all_gather.26
  115.3 9.8 %all_gather.25 = s32[8,1,2,6]{3,2,1,0:T(2,128)S(1)} all-gather(s32[1,1,2,6]{3,2,1,0:T(2,128)} %param.9), channel_id=1, replica_groups=mesh['row'=8,'col'=16,'layer'=2] {'row'}, dimensions={0}, use_global_device_ids=true | all-gather | bytes 432 | tf_op jit(solution)/shard_map/all_gather | solution.py:53
  125.1 58.2 %all_gather.22 = s32[1,32,2,6]{3,2,0,1:T(2,128)S(1)} all-gather(s32[1,1,2,6]{3,2,0,1:T(2,128)} %bitcast.51), channel_id=1, replica_groups=mesh['row'=8,'col'=16,'layer'=2] {'col','layer'}, dimensions={1}, use_global_device_ids=true | all-gather | bytes 1584 | tf_op jit(solution)/shard_map/all_gather | solution.py:91
  183.6 412.7 %all-gather.3.cloned.1.call-done = f32[1,32,2,6,128,128]{5,4,3,2,0,1:T(8,128)} async-done(((f32[1,1,2,6,128,128]{5,4,3,2,0,1:T(8,128)}), f32[1,32,2,6,128,128]{5,4,3,2,0,1:T(8,128)}) %all-gather.3.cloned.1.call-update) | async-done | bytes 25165840 | tf_op jit(solution)/shard_map/all_gather | solution.py:90
  596.3 290.3 %while.12 = (s32[]{:T(128)}, f32[12,128,128]{2,1,0:T(8,128)S(1)}, pred[32,12]{1,0:T(8,128)(4,1)S(1)}, s32[32,12]{1,0:T(8,128)S(1)}, s32[12]{0:T(128)S(1)}, /*ind...) while((s32[]{:T(128)}, f32[12,128,128]{2,1,0:T(8,128)S(1)}, ...), condition=%wide.wide.region_5.6_spmd.clone, body=%wide.wide.region_0.5_spmd.clone.sunk | while | flops 302997888 | bytes 7876635 | solution.py:72
  598.6 3.4 gather_fusion.1
  607.6 3.4 gather_fusion.1
  616.7 3.4 gather_fusion.1
  625.8 3.4 gather_fusion.1
  634.9 3.4 gather_fusion.1
  643.9 3.4 gather_fusion.1
  653.0 3.4 gather_fusion.1
  662.1 3.4 gather_fusion.1
  671.2 3.4 gather_fusion.1
  680.2 3.4 gather_fusion.1
  689.3 3.4 gather_fusion.1
  698.4 3.4 gather_fusion.1
  707.4 3.4 gather_fusion.1
  716.5 3.4 gather_fusion.1
  725.6 3.4 gather_fusion.1
  734.7 3.4 gather_fusion.1
  743.7 3.4 gather_fusion.1
  752.8 3.4 gather_fusion.1
  761.9 3.4 gather_fusion.1
  771.0 3.4 gather_fusion.1
  798.2 3.4 gather_fusion.1
  816.3 3.4 gather_fusion.1
  861.7 3.4 gather_fusion.1
  879.8 3.4 gather_fusion.1
  (642 shorter events, 211.6 us)
Async XLA Ops:
  6.5 177.0 %all-gather.5.cloned.1.call-start = ((), (), s32[]{:S(2)}) async-start(), calls=%async_computation.2 | async-start | bytes 7077888 | tf_op jit(solution)/shard_map/all_gather | solution.py:53
  7.3 589.0 %all-gather.3.cloned.1.call-start = ((), (), s32[]{:S(2)}) async-start(), calls=%async_computation.1 | async-start | bytes 25952256 | tf_op jit(solution)/shard_map/all_gather | solution.py:90
  9.3 174.2 %all-to-all-start = ((s32[32,1,1,2,6]{4,3,2,1,0:T(2,128)}), s32[32,1,1,2,6]{4,3,2,1,0:T(2,128)S(1)}, u32[]{:S(2)}, u32[]{:S(2)}) async-start(s32[32,1,1,2,6]{4,3,2,1,0:T(2,128)} %stack.2), calls=%async_computation | async-start | bytes 65536 | tf_op jit(solution)/shard_map/all_to_all | solution.py:93
  115.2 481.1 %copy-start.1 = (s32[8,1,2,6]{3,2,1,0:T(2,128)}, s32[8,1,2,6]{3,2,1,0:T(2,128)S(1)}, u32[]{:S(2)}) copy-start(s32[8,1,2,6]{3,2,1,0:T(2,128)S(1)} %all_gather.26) | copy-start | bytes 1156
  125.0 471.2 %copy-start.2 = (s32[8,1,2,6]{3,2,1,0:T(2,128)}, s32[8,1,2,6]{3,2,1,0:T(2,128)S(1)}, u32[]{:S(2)}) copy-start(s32[8,1,2,6]{3,2,1,0:T(2,128)S(1)} %all_gather.25) | copy-start | bytes 1156
  886.6 0.9 copy-start
Sparse Core Ops, SparseCore 0:
  9.2 47.6 all-gather.4
  58.7 537.4 all-gather.2
